TPU v7x, 256 devices: a whole 4x4x8 slice. The times are simulated.
256 devices in a mesh: row: 8 (over y, z_lo), col: 32 (over x, z_hi, core).
Axes of the slice: x: 4, y: 4, z: 8 (z_hi: 4, z_lo: 2; z = z_hi * 2 + z_lo), core: 2. Of those that a mesh axis runs over, the one named last changes fastest.
Arguments:
- features: bfloat16 [32768, 128], P(('col', 'row')), may hold values from -6 to 6
- weight: bfloat16 [128, 256], replicated, may hold values from -0.5 to 0.5
- history: bfloat16 [32768, 256], P(('col', 'row')), may hold values from -6 to 6
- in_batch: int32 [32768], P(('col', 'row')), may hold values 0 or 1
- tile_values: bfloat16 [8, 32, 192, 128, 128], P('row', 'col'), as said below
- tile_pos: int32 [8, 32, 192, 2], P('row', 'col'), may hold values from 0 to 31, as said below
- tile_count: int32 [8, 32], P('row', 'col'), may hold values from 1 to 192, as said below
- cotangent: bfloat16 [32768, 256], P(('row', 'col')), may hold values from -6 to 6
Outputs:
- output: bfloat16 [32768, 256], P(('row', 'col'))
- grad_features: bfloat16 [32768, 128], P(('col', 'row'))
- grad_weight: float32 [128, 256], replicated
Inputs may be any that keep to these rules, and one draw needn't show every extreme that they name: tile_pos[..., 0] lies in 0 to 128 * 32 / 128 - 1 and tile_pos[..., 1] in 0 to 128 * 8 / 128 - 1. `tile_count`: at least one block uses all 192 slots. `tile_values`: entries are nonnegative.
All inputs are finite; a program needn't handle non-finite values. No bound on the sum of `in_batch` on one device may be relied on, other than what follows from the above.
Results may differ from a plain program's by a relative error of at most 0.006.
Values may be sent and summed in bfloat16 or wider, within the bound.
No kernel may reach another device: no remote copies, remote signals or barrier semaphores. Data moves between devices by JAX's collectives and lax.ppermute only.
A program may use at most 128 MiB of HBM per device.

v0:
```python
import math
import jax
import jax.numpy as jnp
from jax import lax
from jax.sharding import PartitionSpec as P


def gelu_form(values):
    return jax.nn.gelu(values, approximate=True)


def tile_sweep(group_step, start_value, tiles, coords, valid):
    total_slots = tiles.shape[0]
    group = math.gcd(total_slots, 64)
    tiles_grouped = tiles.reshape(total_slots // group, group, tiles.shape[1], tiles.shape[2])
    coords_grouped = coords.reshape(total_slots // group, group, 2)
    valid_grouped = valid.reshape(total_slots // group, group)

    def scan_step(running, pieces):
        return (group_step(running, pieces[0], pieces[1], pieces[2]), None)

    result, _ = lax.scan(scan_step, start_value, (tiles_grouped, coords_grouped, valid_grouped))
    return result


def body(features, weight, history, in_batch, tile_values, tile_pos, tile_count, cotangent):
    node_count = features.shape[0]
    width = weight.shape[1]
    rows_size = lax.axis_size("row")
    cols_size = lax.axis_size("col")
    block_rows = node_count * cols_size
    block_cols = node_count * rows_size
    tiles = tile_values.reshape(tile_values.shape[2], tile_values.shape[3], tile_values.shape[4])
    coords = tile_pos.reshape(tile_pos.shape[2], 2)
    count = tile_count.reshape(())
    valid = (jnp.arange(tiles.shape[0], dtype=jnp.int32) < count).astype(jnp.float32)
    projected = jnp.dot(features, weight, preferred_element_type=jnp.float32).astype(jnp.bfloat16)
    mixed = jnp.where(in_batch[:, None] == 1, projected, history)
    panel = lax.all_gather(mixed, "row", axis=0, tiled=True)
    panel_tiles = panel.reshape(block_cols // 128, 128, width)

    def forward_group(running, tiles_part, coords_part, valid_part):
        picked = panel_tiles[coords_part[:, 1]]
        product = jnp.einsum("tij,tjh->tih", tiles_part, picked, preferred_element_type=jnp.float32)
        product = product * valid_part[:, None, None]
        return running + jax.ops.segment_sum(
            product, coords_part[:, 0], num_segments=block_rows // 128
        )

    forward_start = jnp.zeros((block_rows // 128, 128, width), jnp.float32)
    partial_rows = tile_sweep(forward_group, forward_start, tiles, coords, valid).reshape(
        block_rows, width
    )
    total = lax.psum_scatter(partial_rows, "col", scatter_dimension=0, tiled=True)
    output = gelu_form(total).astype(jnp.bfloat16)
    _, pullback = jax.vjp(gelu_form, total)
    grad_total = pullback(cotangent.astype(jnp.float32))[0].astype(jnp.bfloat16)
    grad_rows = lax.all_gather(grad_total, "col", axis=0, tiled=True)
    grad_tiles = grad_rows.reshape(block_rows // 128, 128, width)

    def backward_group(running, tiles_part, coords_part, valid_part):
        picked = grad_tiles[coords_part[:, 0]]
        product = jnp.einsum("tij,tih->tjh", tiles_part, picked, preferred_element_type=jnp.float32)
        product = product * valid_part[:, None, None]
        return running + jax.ops.segment_sum(
            product, coords_part[:, 1], num_segments=block_cols // 128
        )

    backward_start = jnp.zeros((block_cols // 128, 128, width), jnp.float32)
    partial_cols = tile_sweep(backward_group, backward_start, tiles, coords, valid).reshape(
        block_cols, width
    )
    grad_mixed = lax.psum_scatter(partial_cols, "row", scatter_dimension=0, tiled=True)
    grad_projected = (grad_mixed * in_batch[:, None].astype(jnp.float32)).astype(jnp.bfloat16)
    grad_features = jnp.dot(grad_projected, weight.T, preferred_element_type=jnp.float32).astype(
        jnp.bfloat16
    )
    weight_term = jnp.dot(features.T, grad_projected, preferred_element_type=jnp.float32)
    weight_total = lax.psum(weight_term, ("row", "col"))
    scale_factor = 1.0 / math.sqrt(node_count * rows_size * cols_size)
    grad_weight = weight_total * jnp.float32(scale_factor)
    return (output, grad_features, grad_weight)


def solution(mesh):
    in_specs = (
        P(("col", "row"), None),
        P(),
        P(("col", "row"), None),
        P(("col", "row")),
        P("row", "col", None, None, None),
        P("row", "col", None, None),
        P("row", "col"),
        P(("row", "col"), None),
    )
    out_specs = (P(("row", "col"), None), P(("col", "row"), None), P())
    return jax.shard_map(body, mesh=mesh, in_specs=in_specs, out_specs=out_specs, check_vma=False)
```

profile of v0, /device:TPU:2, one launch (start us, length us, event | category | flops | bytes accessed | tf_op | source)
XLA Modules:
  0.0 661.4 jit_solution(3899024853442598339)
XLA Ops:
  9.3 1.0 fusion.10
  10.3 30.2 %all_gather.6 = bf16[1024,256]{1,0:T(8,128)(2,1)S(1)} all-gather(bf16[128,256]{1,0:T(8,128)(2,1)S(1)} %fusion.10), channel_id=1, replica_groups=mesh['row'=8,'col'=32] {'row'}, dimensions={0}, use_global_device_ids=true | all-gather | bytes 589824 | tf_op jit(solution)/shard_map/all_gather | solution.py:39
  40.5 2.4 broadcast.43
  42.9 87.8 %while.20 = (s32[]{:T(128)}, f32[32,128,256]{2,1,0:T(8,128)}, s32[3,64,2]{1,2,0:T(2,128)S(1)}, bf16[3,64,128,128]{3,2,1,0:T(8,128)(2,1)}, bf16[8,128,256]{2,1,0:...) while((s32[]{:T(128)}, f32[32,128,256]{2,1,0:T(8,128)}, s32[3,64,2]{1,2,0:T(2,128)S(1)}, ...), condition=%wide.region_2.3_spmd, body=%wide.region_0.2_spmd.sunk | while | flops 541066432 | bytes 48242772 | solution.py:22
  43.0 2.8 gather_fusion
  45.7 7.3 %broadcast_multiply_fusion.5 = f32[64,128,256]{2,1,0:T(8,128)} fusion(f32[64]{0:T(128)S(1)} %fusion.39, bf16[64,128,256]{2,1,0:T(8,128)(2,1)} %gather_fusion, bf16[3,64,128,128]{3,2,1,0:T(8,128)(2,1)} %get-tuple-element.222, s32[]{:T(128)} %get-tuple-element.212), kind=kOutput, calls=%fused_computation.4.clone.1 | convolution fusion | flops 538968064 | bytes 14680832 | tf_op jit(solution)/shard_map/while/body/eval_jaxpr/tij,tjh->tih/dot_general | solution.py:44
  53.0 19.1 %scatter_fusion = f32[32,128,256]{2,1,0:T(8,128)} fusion(f32[32,128,256]{2,1,0:T(8,128)} %get-tuple-element.213, s32[64]{0:T(128)S(1)} %get-tuple-element.195, f32[64,128,256]{2,1,0:T(8,128)} %broadcast_multiply_fusion.5), kind=kCustom, calls=%fused_computation.2.clone.1 | custom fusion | flops 2097152 | bytes 25166080 | tf_op jit(solution)/shard_map/while/body/eval_jaxpr/scatter-add | solution.py:46
  72.2 2.8 gather_fusion
  75.0 7.3 %broadcast_multiply_fusion.5 = f32[64,128,256]{2,1,0:T(8,128)} fusion(f32[64]{0:T(128)S(1)} %fusion.39, bf16[64,128,256]{2,1,0:T(8,128)(2,1)} %gather_fusion, bf16[3,64,128,128]{3,2,1,0:T(8,128)(2,1)} %get-tuple-element.222, s32[]{:T(128)} %get-tuple-element.212), kind=kOutput, calls=%fused_computation.4.clone.1 | convolution fusion | flops 538968064 | bytes 14680832 | tf_op jit(solution)/shard_map/while/body/eval_jaxpr/tij,tjh->tih/dot_general | solution.py:44
  82.3 19.3 %scatter_fusion = f32[32,128,256]{2,1,0:T(8,128)} fusion(f32[32,128,256]{2,1,0:T(8,128)} %get-tuple-element.213, s32[64]{0:T(128)S(1)} %get-tuple-element.195, f32[64,128,256]{2,1,0:T(8,128)} %broadcast_multiply_fusion.5), kind=kCustom, calls=%fused_computation.2.clone.1 | custom fusion | flops 2097152 | bytes 25166080 | tf_op jit(solution)/shard_map/while/body/eval_jaxpr/scatter-add | solution.py:46
  101.6 2.8 gather_fusion
  104.3 7.3 %broadcast_multiply_fusion.5 = f32[64,128,256]{2,1,0:T(8,128)} fusion(f32[64]{0:T(128)S(1)} %fusion.39, bf16[64,128,256]{2,1,0:T(8,128)(2,1)} %gather_fusion, bf16[3,64,128,128]{3,2,1,0:T(8,128)(2,1)} %get-tuple-element.222, s32[]{:T(128)} %get-tuple-element.212), kind=kOutput, calls=%fused_computation.4.clone.1 | convolution fusion | flops 538968064 | bytes 14680832 | tf_op jit(solution)/shard_map/while/body/eval_jaxpr/tij,tjh->tih/dot_general | solution.py:44
  111.6 19.1 %scatter_fusion = f32[32,128,256]{2,1,0:T(8,128)} fusion(f32[32,128,256]{2,1,0:T(8,128)} %get-tuple-element.213, s32[64]{0:T(128)S(1)} %get-tuple-element.195, f32[64,128,256]{2,1,0:T(8,128)} %broadcast_multiply_fusion.5), kind=kCustom, calls=%fused_computation.2.clone.1 | custom fusion | flops 2097152 | bytes 25166080 | tf_op jit(solution)/shard_map/while/body/eval_jaxpr/scatter-add | solution.py:46
  130.9 101.0 %reduce-scatter.3.cloned.1.call-done = f32[128,256]{1,0:T(8,128)} async-done(((f32[4096,256]{1,0:T(8,128)}), f32[128,256]{1,0:T(8,128)}) %reduce-scatter.3.cloned.1.call-update) | async-done | bytes 131088 | tf_op jit(solution)/shard_map/reduce_scatter | solution.py:54
  231.8 1.7 fusion.13
  233.6 8.6 %copy.14 = bf16[1,1,192,128,128]{3,4,2,1,0:T(8,128)(2,1)} copy(bf16[1,1,192,128,128]{4,3,2,1,0:T(8,128)(2,1)} %bitcast.65) | data formatting | bytes 12582912 | tf_op args[4]
  242.1 45.0 %all-gather.2.cloned.1.call-done = bf16[4096,256]{1,0:T(8,128)(2,1)} async-done(((bf16[128,256]{1,0:T(8,128)(2,1)}), bf16[4096,256]{1,0:T(8,128)(2,1)}) %all-gather.2.cloned.1.call-update) | async-done | bytes 2097168 | tf_op jit(solution)/shard_map/all_gather | solution.py:58
  287.3 72.3 %while.21 = (s32[]{:T(128)}, f32[8,128,256]{2,1,0:T(8,128)S(1)}, s32[3,64,2]{1,2,0:T(2,128)S(1)}, bf16[3,64,128,128]{2,3,1,0:T(8,128)(2,1)}, bf16[32,128,256]{2,...) while((s32[]{:T(128)}, f32[8,128,256]{2,1,0:T(8,128)S(1)}, s32[3,64,2]{1,2,0:T(2,128)S(1)}, ...), condition=%wide.region_6.7_spmd, body=%wide.region_4.6_spmd.sunk | while | flops 541066432 | bytes 48242772 | solution.py:22
  287.3 4.4 gather_fusion.1
  291.7 7.3 %broadcast_multiply_fusion.6 = f32[64,128,256]{2,1,0:T(8,128)} fusion(f32[64]{0:T(128)S(1)} %fusion.43, bf16[64,128,256]{2,1,0:T(8,128)(2,1)} %gather_fusion.1, bf16[3,64,128,128]{2,3,1,0:T(8,128)(2,1)} %get-tuple-element.243, s32[]{:T(128)} %get-tuple-element.233), kind=kOutput, calls=%fused_computation.15.clone.1 | convolution fusion | flops 538968064 | bytes 14680832 | tf_op jit(solution)/shard_map/while/body/eval_jaxpr/tij,tih->tjh/dot_general | solution.py:63
  299.0 12.4 %scatter_fusion.1 = f32[8,128,256]{2,1,0:T(8,128)S(1)} fusion(f32[8,128,256]{2,1,0:T(8,128)S(1)} %get-tuple-element.234, s32[64]{0:T(128)S(1)} %get-tuple-element.203, f32[64,128,256]{2,1,0:T(8,128)} %broadcast_multiply_fusion.6), kind=kCustom, calls=%fused_computation.3.clone.1 | custom fusion | flops 2097152 | bytes 25166080 | tf_op jit(solution)/shard_map/while/body/eval_jaxpr/scatter-add | solution.py:65
  311.5 4.4 gather_fusion.1
  315.8 7.3 %broadcast_multiply_fusion.6 = f32[64,128,256]{2,1,0:T(8,128)} fusion(f32[64]{0:T(128)S(1)} %fusion.43, bf16[64,128,256]{2,1,0:T(8,128)(2,1)} %gather_fusion.1, bf16[3,64,128,128]{2,3,1,0:T(8,128)(2,1)} %get-tuple-element.243, s32[]{:T(128)} %get-tuple-element.233), kind=kOutput, calls=%fused_computation.15.clone.1 | convolution fusion | flops 538968064 | bytes 14680832 | tf_op jit(solution)/shard_map/while/body/eval_jaxpr/tij,tih->tjh/dot_general | solution.py:63
  323.1 12.4 %scatter_fusion.1 = f32[8,128,256]{2,1,0:T(8,128)S(1)} fusion(f32[8,128,256]{2,1,0:T(8,128)S(1)} %get-tuple-element.234, s32[64]{0:T(128)S(1)} %get-tuple-element.203, f32[64,128,256]{2,1,0:T(8,128)} %broadcast_multiply_fusion.6), kind=kCustom, calls=%fused_computation.3.clone.1 | custom fusion | flops 2097152 | bytes 25166080 | tf_op jit(solution)/shard_map/while/body/eval_jaxpr/scatter-add | solution.py:65
  335.6 4.4 gather_fusion.1
  339.9 7.3 %broadcast_multiply_fusion.6 = f32[64,128,256]{2,1,0:T(8,128)} fusion(f32[64]{0:T(128)S(1)} %fusion.43, bf16[64,128,256]{2,1,0:T(8,128)(2,1)} %gather_fusion.1, bf16[3,64,128,128]{2,3,1,0:T(8,128)(2,1)} %get-tuple-element.243, s32[]{:T(128)} %get-tuple-element.233), kind=kOutput, calls=%fused_computation.15.clone.1 | convolution fusion | flops 538968064 | bytes 14680832 | tf_op jit(solution)/shard_map/while/body/eval_jaxpr/tij,tih->tjh/dot_general | solution.py:63
  347.2 12.4 %scatter_fusion.1 = f32[8,128,256]{2,1,0:T(8,128)S(1)} fusion(f32[8,128,256]{2,1,0:T(8,128)S(1)} %get-tuple-element.234, s32[64]{0:T(128)S(1)} %get-tuple-element.203, f32[64,128,256]{2,1,0:T(8,128)} %broadcast_multiply_fusion.6), kind=kCustom, calls=%fused_computation.3.clone.1 | custom fusion | flops 2097152 | bytes 25166080 | tf_op jit(solution)/shard_map/while/body/eval_jaxpr/scatter-add | solution.py:65
  359.6 1.0 copy-done.1
  360.7 42.6 %reduce-scatter.5.cloned.1.call-done = f32[128,256]{1,0:T(8,128)} async-done(((f32[1024,256]{1,0:T(8,128)}), f32[128,256]{1,0:T(8,128)}) %reduce-scatter.5.cloned.1.call-update) | async-done | bytes 131088 | tf_op jit(solution)/shard_map/reduce_scatter | solution.py:73
  403.3 1.8 convolution_bitcast_fusion
  405.1 1.7 convolution_convert_fusion.1
  406.9 246.3 %all-reduce.2.cloned.1.call-done = f32[128,256]{0,1:T(8,128)} async-done(((f32[128,256]{0,1:T(8,128)}), f32[128,256]{0,1:T(8,128)}) %all-reduce.2.cloned.1.call-update) | async-done | bytes 131088 | tf_op jit(solution)/shard_map/psum | solution.py:79
  (49 shorter events, 3.6 us)
Async XLA Ops:
  7.2 2.2 copy-start
  7.2 224.6 %reduce-scatter.3.cloned.1.call-start = ((), (), s32[]{:S(2)}) async-start(), calls=%async_computation.2 | async-start | bytes 4325376 | tf_op jit(solution)/shard_map/reduce_scatter | solution.py:54
  130.8 101.0 %copy-start.3 = (bf16[128,256]{1,0:T(8,128)(2,1)S(1)}, bf16[128,256]{1,0:T(8,128)(2,1)}, u32[]{:S(2)}) copy-start(bf16[128,256]{1,0:T(8,128)(2,1)} %param.19) | copy-start | bytes 196612
  130.8 156.4 %all-gather.2.cloned.1.call-start = ((), (), s32[]{:S(2)}) async-start(), calls=%async_computation.3 | async-start | bytes 2162688 | tf_op jit(solution)/shard_map/all_gather | solution.py:58
  233.5 169.8 %reduce-scatter.5.cloned.1.call-start = ((), (), s32[]{:S(2)}) async-start(), calls=%async_computation.4 | async-start | bytes 1179648 | tf_op jit(solution)/shard_map/reduce_scatter | solution.py:73
  287.3 73.4 %copy-start.4 = (s32[128]{0:T(128)S(1)}, s32[128]{0:T(128)}, u32[]{:S(2)}) copy-start(s32[128]{0:T(128)} %param.15) | copy-start | bytes 1540
  287.3 116.0 %copy-start.2 = (bf16[128,128]{1,0:T(8,128)(2,1)S(1)}, bf16[128,128]{1,0:T(8,128)(2,1)}, u32[]{:S(2)}) copy-start(bf16[128,128]{1,0:T(8,128)(2,1)} %param.12) | copy-start | bytes 98308
  359.6 1.0 copy-start.1
  360.6 292.6 %all-reduce.2.cloned.1.call-start = ((), (), s32[]{:S(2)}) async-start(), calls=%async_computation.5 | async-start | bytes 262144 | tf_op jit(solution)/shard_map/psum | solution.py:79
Sparse Core Ops, SparseCore 0:
  130.9 100.8 reduce-scatter.2
  235.0 52.1 all-gather.1
  360.7 42.4 reduce-scatter.4
  409.2 243.9 all-reduce.1
where the time goes:
time: 662 us; the launch traced here: 661 us
  waiting for transfers between devices  435 us (66%)
  other arithmetic  98 us (15%)
  matrix products  48.4 us (7%)
  local copies, waits for them, and re-layouts  35.1 us (5%)
  blocking collectives  30.2 us (5%)
  between operations  14.5 us (2%)
    psum x1, waiting for transfers between devices, body(): weight_total = lax.psum(weight_term, ('row', 'col'))  246 us
    reduce_scatter x1, waiting for transfers between devices, body(): lax.psum_scatter(partial_rows, 'col', scatter_dimension=0, tiled=True)  101 us
    scatter-add x3, other arithmetic, forward_group(): jax.ops.segment_sum(product, coords_part[:, 0], num_segments=block_rows /...  57.5 us
    all_gather x1, waiting for transfers between devices, body(): grad_rows = lax.all_gather(grad_total, 'col', axis=0, tiled=True)  45 us
    reduce_scatter x1, waiting for transfers between devices, body(): lax.psum_scatter(partial_cols, 'row', scatter_dimension=0, tiled=True)  42.6 us
    scatter-add x3, other arithmetic, backward_group(): jax.ops.segment_sum(product, coords_part[:, 1], num_segments=block_cols /...  37.1 us
    all_gather x1, blocking collectives, body(): panel = lax.all_gather(mixed, 'row', axis=0, tiled=True)  30.2 us
    dot_general x3, matrix products, forward_group(): jnp.einsum('tij,tjh->tih', tiles_part, picked, preferred_element_type=jnp...  21.9 us
  transfers between devices with their start and end apart: 4, of which 4 were waited for; matrix products, arithmetic and copies ran while one was open for 2% of the time, Pallas kernels for 0%

commit v1 on v0

--- a/solution.py
+++ b/solution.py
@@ -76,7 +76,7 @@
         jnp.bfloat16
     )
     weight_term = jnp.dot(features.T, grad_projected, preferred_element_type=jnp.float32)
-    weight_total = lax.psum(weight_term, ("row", "col"))
+    weight_total = lax.psum(lax.psum(weight_term, "col"), "row")
     scale_factor = 1.0 / math.sqrt(node_count * rows_size * cols_size)
     grad_weight = weight_total * jnp.float32(scale_factor)
     return (output, grad_features, grad_weight)

time: 662 us -> 755 us (1.14)
  waiting for transfers between devices: 435 us -> 527 us
    psum x1 -> x2, waiting for transfers between devices: 246 us -> 339 us  [body(): weight_total = lax.psum(lax.psum(weight_term, 'col'), 'row')]
  transfers between devices with their start and end apart: 4 -> 5, of which waited for: 4 -> 5; matrix products, arithmetic and copies ran while one was open for 2% -> 1% of each run, Pallas kernels for 0% -> 0%
where the time goes in v1:
time: 755 us; the launch traced here: 754 us
  waiting for transfers between devices  527 us (70%)
  other arithmetic  98 us (13%)
  matrix products  48.4 us (6%)
  local copies, waits for them, and re-layouts  35.1 us (5%)
  blocking collectives  30.2 us (4%)
  between operations  14.5 us (2%)
    psum x2, waiting for transfers between devices, body(): weight_total = lax.psum(lax.psum(weight_term, 'col'), 'row')  339 us
    reduce_scatter x1, waiting for transfers between devices, body(): lax.psum_scatter(partial_rows, 'col', scatter_dimension=0, tiled=True)  101 us
    scatter-add x3, other arithmetic, forward_group(): jax.ops.segment_sum(product, coords_part[:, 0], num_segments=block_rows /...  57.5 us
    all_gather x1, waiting for transfers between devices, body(): grad_rows = lax.all_gather(grad_total, 'col', axis=0, tiled=True)  45 us
    reduce_scatter x1, waiting for transfers between devices, body(): lax.psum_scatter(partial_cols, 'row', scatter_dimension=0, tiled=True)  42.6 us
    scatter-add x3, other arithmetic, backward_group(): jax.ops.segment_sum(product, coords_part[:, 1], num_segments=block_cols /...  37.1 us
    all_gather x1, blocking collectives, body(): panel = lax.all_gather(mixed, 'row', axis=0, tiled=True)  30.2 us
    dot_general x3, matrix products, forward_group(): jnp.einsum('tij,tjh->tih', tiles_part, picked, preferred_element_type=jnp...  21.9 us
  transfers between devices with their start and end apart: 5, of which 5 were waited for; matrix products, arithmetic and copies ran while one was open for 1% of the time, Pallas kernels for 0%

profile of v1, /device:TPU:2, one launch (start us, length us, event | category | flops | bytes accessed | tf_op | source)
XLA Modules:
  0.0 754.0 jit_solution(8574432269257557413)
XLA Ops:
  9.3 1.0 fusion.10
  10.3 30.2 %all_gather.6 = bf16[1024,256]{1,0:T(8,128)(2,1)S(1)} all-gather(bf16[128,256]{1,0:T(8,128)(2,1)S(1)} %fusion.10), channel_id=1, replica_groups=mesh['row'=8,'col'=32] {'row'}, dimensions={0}, use_global_device_ids=true | all-gather | bytes 589824 | tf_op jit(solution)/shard_map/all_gather | solution.py:39
  40.5 2.4 broadcast.43
  42.9 87.8 %while.20 = (s32[]{:T(128)}, f32[32,128,256]{2,1,0:T(8,128)}, s32[3,64,2]{1,2,0:T(2,128)S(1)}, bf16[3,64,128,128]{3,2,1,0:T(8,128)(2,1)}, bf16[8,128,256]{2,1,0:...) while((s32[]{:T(128)}, f32[32,128,256]{2,1,0:T(8,128)}, s32[3,64,2]{1,2,0:T(2,128)S(1)}, ...), condition=%wide.region_2.3_spmd, body=%wide.region_0.2_spmd.sunk | while | flops 541066432 | bytes 48242772 | solution.py:22
  43.0 2.8 gather_fusion
  45.7 7.3 broadcast_multiply_fusion.5
  53.0 19.1 %scatter_fusion = f32[32,128,256]{2,1,0:T(8,128)} fusion(f32[32,128,256]{2,1,0:T(8,128)} %get-tuple-element.213, s32[64]{0:T(128)S(1)} %get-tuple-element.195, f32[64,128,256]{2,1,0:T(8,128)} %broadcast_multiply_fusion.5), kind=kCustom, calls=%fused_computation.2.clone.1 | custom fusion | flops 2097152 | bytes 25166080 | tf_op jit(solution)/shard_map/while/body/eval_jaxpr/scatter-add | solution.py:46
  72.2 2.8 gather_fusion
  75.0 7.3 broadcast_multiply_fusion.5
  82.3 19.3 %scatter_fusion = f32[32,128,256]{2,1,0:T(8,128)} fusion(f32[32,128,256]{2,1,0:T(8,128)} %get-tuple-element.213, s32[64]{0:T(128)S(1)} %get-tuple-element.195, f32[64,128,256]{2,1,0:T(8,128)} %broadcast_multiply_fusion.5), kind=kCustom, calls=%fused_computation.2.clone.1 | custom fusion | flops 2097152 | bytes 25166080 | tf_op jit(solution)/shard_map/while/body/eval_jaxpr/scatter-add | solution.py:46
  101.6 2.8 gather_fusion
  104.3 7.3 broadcast_multiply_fusion.5
  111.6 19.1 %scatter_fusion = f32[32,128,256]{2,1,0:T(8,128)} fusion(f32[32,128,256]{2,1,0:T(8,128)} %get-tuple-element.213, s32[64]{0:T(128)S(1)} %get-tuple-element.195, f32[64,128,256]{2,1,0:T(8,128)} %broadcast_multiply_fusion.5), kind=kCustom, calls=%fused_computation.2.clone.1 | custom fusion | flops 2097152 | bytes 25166080 | tf_op jit(solution)/shard_map/while/body/eval_jaxpr/scatter-add | solution.py:46
  130.9 101.0 %reduce-scatter.3.cloned.1.call-done = f32[128,256]{1,0:T(8,128)} async-done(((f32[4096,256]{1,0:T(8,128)}), f32[128,256]{1,0:T(8,128)}) %reduce-scatter.3.cloned.1.call-update) | async-done | bytes 131088 | tf_op jit(solution)/shard_map/reduce_scatter | solution.py:54
  231.8 1.7 fusion.13
  233.6 8.6 %copy.14 = bf16[1,1,192,128,128]{3,4,2,1,0:T(8,128)(2,1)} copy(bf16[1,1,192,128,128]{4,3,2,1,0:T(8,128)(2,1)} %bitcast.65) | data formatting | bytes 12582912 | tf_op args[4]
  242.1 45.0 %all-gather.2.cloned.1.call-done = bf16[4096,256]{1,0:T(8,128)(2,1)} async-done(((bf16[128,256]{1,0:T(8,128)(2,1)}), bf16[4096,256]{1,0:T(8,128)(2,1)}) %all-gather.2.cloned.1.call-update) | async-done | bytes 2097168 | tf_op jit(solution)/shard_map/all_gather | solution.py:58
  287.3 72.3 %while.21 = (s32[]{:T(128)}, f32[8,128,256]{2,1,0:T(8,128)S(1)}, s32[3,64,2]{1,2,0:T(2,128)S(1)}, bf16[3,64,128,128]{2,3,1,0:T(8,128)(2,1)}, bf16[32,128,256]{2,...) while((s32[]{:T(128)}, f32[8,128,256]{2,1,0:T(8,128)S(1)}, s32[3,64,2]{1,2,0:T(2,128)S(1)}, ...), condition=%wide.region_6.7_spmd, body=%wide.region_4.6_spmd.sunk | while | flops 541066432 | bytes 48242772 | solution.py:22
  287.3 4.4 gather_fusion.1
  291.7 7.3 broadcast_multiply_fusion.6
  299.0 12.4 %scatter_fusion.1 = f32[8,128,256]{2,1,0:T(8,128)S(1)} fusion(f32[8,128,256]{2,1,0:T(8,128)S(1)} %get-tuple-element.234, s32[64]{0:T(128)S(1)} %get-tuple-element.203, f32[64,128,256]{2,1,0:T(8,128)} %broadcast_multiply_fusion.6), kind=kCustom, calls=%fused_computation.3.clone.1 | custom fusion | flops 2097152 | bytes 25166080 | tf_op jit(solution)/shard_map/while/body/eval_jaxpr/scatter-add | solution.py:65
  311.5 4.4 gather_fusion.1
  315.8 7.3 broadcast_multiply_fusion.6
  323.1 12.4 %scatter_fusion.1 = f32[8,128,256]{2,1,0:T(8,128)S(1)} fusion(f32[8,128,256]{2,1,0:T(8,128)S(1)} %get-tuple-element.234, s32[64]{0:T(128)S(1)} %get-tuple-element.203, f32[64,128,256]{2,1,0:T(8,128)} %broadcast_multiply_fusion.6), kind=kCustom, calls=%fused_computation.3.clone.1 | custom fusion | flops 2097152 | bytes 25166080 | tf_op jit(solution)/shard_map/while/body/eval_jaxpr/scatter-add | solution.py:65
  335.6 4.4 gather_fusion.1
  339.9 7.3 broadcast_multiply_fusion.6
  347.2 12.4 %scatter_fusion.1 = f32[8,128,256]{2,1,0:T(8,128)S(1)} fusion(f32[8,128,256]{2,1,0:T(8,128)S(1)} %get-tuple-element.234, s32[64]{0:T(128)S(1)} %get-tuple-element.203, f32[64,128,256]{2,1,0:T(8,128)} %broadcast_multiply_fusion.6), kind=kCustom, calls=%fused_computation.3.clone.1 | custom fusion | flops 2097152 | bytes 25166080 | tf_op jit(solution)/shard_map/while/body/eval_jaxpr/scatter-add | solution.py:65
  360.7 42.6 %reduce-scatter.5.cloned.1.call-done = f32[128,256]{1,0:T(8,128)} async-done(((f32[1024,256]{1,0:T(8,128)}), f32[128,256]{1,0:T(8,128)}) %reduce-scatter.5.cloned.1.call-update) | async-done | bytes 131088 | tf_op jit(solution)/shard_map/reduce_scatter | solution.py:73
  403.3 1.8 convolution_bitcast_fusion
  405.2 256.1 %all-reduce.3.cloned.1.call-done = f32[128,256]{0,1:T(8,128)} async-done(((f32[128,256]{0,1:T(8,128)}), f32[128,256]{0,1:T(8,128)}) %all-reduce.3.cloned.1.call-update) | async-done | bytes 131088 | tf_op jit(solution)/shard_map/psum | solution.py:79
  661.3 1.7 convolution_convert_fusion.1
  663.1 82.7 %all-reduce.5.cloned.1.call-done = f32[128,256]{0,1:T(8,128)} async-done(((f32[128,256]{0,1:T(8,128)}), f32[128,256]{0,1:T(8,128)}) %all-reduce.5.cloned.1.call-update) | async-done | bytes 131088 | tf_op jit(solution)/shard_map/psum | solution.py:79
  (52 shorter events, 4.6 us)
Async XLA Ops:
  7.2 2.2 copy-start
  7.2 224.6 %reduce-scatter.3.cloned.1.call-start = ((), (), s32[]{:S(2)}) async-start(), calls=%async_computation.2 | async-start | bytes 4325376 | tf_op jit(solution)/shard_map/reduce_scatter | solution.py:54
  130.8 101.0 %copy-start.3 = (bf16[128,256]{1,0:T(8,128)(2,1)S(1)}, bf16[128,256]{1,0:T(8,128)(2,1)}, u32[]{:S(2)}) copy-start(bf16[128,256]{1,0:T(8,128)(2,1)} %param.19) | copy-start | bytes 196612
  130.8 156.4 %all-gather.2.cloned.1.call-start = ((), (), s32[]{:S(2)}) async-start(), calls=%async_computation.3 | async-start | bytes 2162688 | tf_op jit(solution)/shard_map/all_gather | solution.py:58
  233.5 169.8 %reduce-scatter.5.cloned.1.call-start = ((), (), s32[]{:S(2)}) async-start(), calls=%async_computation.4 | async-start | bytes 1179648 | tf_op jit(solution)/shard_map/reduce_scatter | solution.py:73
  287.3 73.4 %copy-start.4 = (s32[128]{0:T(128)S(1)}, s32[128]{0:T(128)}, u32[]{:S(2)}) copy-start(s32[128]{0:T(128)} %param.15) | copy-start | bytes 1540
  287.3 116.0 %copy-start.2 = (bf16[128,128]{1,0:T(8,128)(2,1)S(1)}, bf16[128,128]{1,0:T(8,128)(2,1)}, u32[]{:S(2)}) copy-start(bf16[128,128]{1,0:T(8,128)(2,1)} %param.12) | copy-start | bytes 98308
  359.6 1.0 copy-start.1
  360.6 300.7 %all-reduce.3.cloned.1.call-start = ((), (), s32[]{:S(2)}) async-start(), calls=%async_computation.5 | async-start | bytes 262144 | tf_op jit(solution)/shard_map/psum | solution.py:79
  405.1 340.6 %all-reduce.5.cloned.1.call-start = ((), (), s32[]{:S(2)}) async-start(), calls=%async_computation.6 | async-start | bytes 262144 | tf_op jit(solution)/shard_map/psum | solution.py:79
Sparse Core Ops, SparseCore 0:
  130.9 100.8 reduce-scatter.2
  235.0 52.1 all-gather.1
  360.7 42.4 reduce-scatter.4
  406.3 254.9 all-reduce.2
  663.8 81.9 all-reduce.4
